TPU v7x, 256 devices: a whole 4x4x8 slice. The times are simulated.
256 devices in a mesh: view: 8 (over y_lo, x), tile: 32 (over y_hi, z, core).
Axes of the slice: x: 4, y: 4 (y_hi: 2, y_lo: 2; y = y_hi * 2 + y_lo), z: 8, core: 2. Of those that a mesh axis runs over, the one named last changes fastest.
Arguments:
- estimate: float32 [1024, 64, 256], P('tile'), may hold values from 0.5 to 2
- measured: bfloat16 [8, 1024, 64, 256], P('view', 'tile'), may hold values from 0.5 to 2
- blur_profile: float32 [8, 256], P('view'), may hold values from 0.1 to 1
- view_offset: int32 [8], P('view'), may hold values from -6 to 6, as said below
- tile_shift: int32 [8], P('view'), may hold values from 0 to 31
Outputs:
- updated: float32 [1024, 64, 256], P('tile')
Inputs may be any that keep to these rules, and one draw needn't show every extreme that they name: `view_offset`: some view has offset 6 and some other view has offset -6.
All inputs are finite; a program needn't handle non-finite values.
Results may differ from a plain program's by a relative error of at most 0.0016.
Values may be sent and summed in bfloat16 or wider, within the bound.
No kernel may reach another device: no remote copies, remote signals or barrier semaphores. Data moves between devices by JAX's collectives and lax.ppermute only.
A program may use at most 64 MiB of HBM per device.

v0:
```python
import math

import jax
import jax.numpy as jnp
from jax import lax
from jax.sharding import PartitionSpec as P

H = 6


profile_sigma = 48.0


def with_halo(cells, sides, width):
    for axis, dim in sides:
        count = lax.axis_size(axis)
        head = lax.slice_in_dim(cells, 0, width, axis=dim)
        tail = lax.slice_in_dim(cells, cells.shape[dim] - width, cells.shape[dim], axis=dim)
        cells = jnp.concatenate(
            [
                lax.ppermute(tail, axis, [(i, (i + 1) % count) for i in range(count)]),
                cells,
                lax.ppermute(head, axis, [((i + 1) % count, i) for i in range(count)]),
            ],
            axis=dim,
        )
    return cells


def from_behind(block, axis, distance):
    devices = range(lax.axis_size(axis))
    route = [((i - distance) % len(devices), i) for i in devices]
    return lax.ppermute(block, axis, route)


def make_kernel(profile):
    length = profile.shape[0]
    column = jnp.arange(length)
    distance = jnp.minimum(column, length - column).astype(jnp.float32)
    weights = profile * jnp.exp(-distance * distance / (2.0 * profile_sigma * profile_sigma))
    return weights / jnp.sum(weights)


def matmul_high(left, right):
    return jnp.dot(left, right, precision=lax.Precision.HIGHEST, preferred_element_type=jnp.float32)


def body(estimate, measured, blur_profile, view_offset, tile_shift):
    view_count = lax.axis_size("view")
    view_index = lax.axis_index("view")
    blend_weight = (view_index + 1).astype(jnp.float32) / (view_count + 1)
    kernel = make_kernel(blur_profile[0])
    offset = view_offset[0]
    tile_move = tile_shift[0]
    length = estimate.shape[2]
    halo_width = H + 1
    bit_count = (lax.axis_size("tile") - 1).bit_length()
    column = jnp.arange(length)
    phase = column[:, None] * column[None, :] % length
    angle = phase.astype(jnp.float32) * (2.0 * math.pi / length)
    cosine = jnp.cos(angle)
    sine_table = jnp.sin(angle)
    spec_real = matmul_high(kernel, cosine)
    spec_imag = -matmul_high(kernel, sine_table)

    def blur_along(volume, adjoint):
        imag_kernel = -spec_imag if adjoint else spec_imag
        real_part = matmul_high(volume, cosine)
        imag_part = -matmul_high(volume, sine_table)
        out_real = real_part * spec_real - imag_part * imag_kernel
        out_imag = real_part * imag_kernel + imag_part * spec_real
        return (matmul_high(out_real, cosine) - matmul_high(out_imag, sine_table)) / length

    relocated = estimate
    for level in range(bit_count):
        stride = 1 << level
        arrived = from_behind(relocated.astype(jnp.bfloat16), "tile", -stride).astype(
            relocated.dtype
        )
        relocated = jnp.where(tile_move // stride % 2 == 1, arrived, relocated)
    padded = with_halo(relocated, (("tile", 0),), halo_width)
    rows = relocated.shape[0]
    first = lax.dynamic_slice_in_dim(padded, halo_width + offset, rows, 0)
    second = lax.dynamic_slice_in_dim(padded, halo_width + offset + 1, rows, 0)
    forward = blur_along(blend_weight * first + (1.0 - blend_weight) * second, False)
    ratios = measured[0].astype(jnp.float32) / forward
    volume = blur_along(ratios, True)
    padded = with_halo(volume, (("tile", 0),), halo_width)
    rows = volume.shape[0]
    first = lax.dynamic_slice_in_dim(padded, halo_width - offset, rows, 0)
    second = lax.dynamic_slice_in_dim(padded, halo_width - offset - 1, rows, 0)
    correction = blend_weight * first + (1.0 - blend_weight) * second
    for level in range(bit_count):
        stride = 1 << level
        arrived = from_behind(correction, "tile", stride)
        correction = jnp.where(tile_move // stride % 2 == 1, arrived, correction)
    log_terms = jnp.log(correction)
    summed = lax.psum(log_terms, "view")
    return estimate * jnp.exp(summed)


def solution(mesh):
    placed = (
        P("tile", None, None),
        P("view", "tile", None, None),
        P("view", None),
        P("view"),
        P("view"),
    )
    return jax.shard_map(
        body, mesh=mesh, in_specs=placed, out_specs=P("tile", None, None), check_vma=False
    )
```

profile of v0, /device:TPU:1, one launch (start us, length us, event | category | flops | bytes accessed | tf_op | source)
XLA Modules:
  0.0 740.4 jit_solution(8670990774222465612)
XLA Ops:
  6.5 2.9 convert_element_type.66
  9.4 3.2 collective-permute-start
  13.3 11.8 %collective-permute-done = bf16[32,64,256]{2,1,0:T(8,128)(2,1)S(1)} collective-permute-done((bf16[32,64,256]{2,1,0:T(8,128)(2,1)}, bf16[32,64,256]{2,1,0:T(8,128)(2,1)S(1)}, u32[]{:S(2)}, u32[]{:S(2)}) %collective-permute-start) | collective-permute-done | bytes 1048608 | tf_op jit(solution)/shard_map/ppermute | solution.py:33
  25.1 1.3 fusion.22
  26.4 11.4 %collective-permute-start.1 = (bf16[32,64,256]{2,1,0:T(8,128)(2,1)}, bf16[32,64,256]{2,1,0:T(8,128)(2,1)}, u32[]{:S(2)}, u32[]{:S(2)}) collective-permute-start(bf16[32,64,256]{2,1,0:T(8,128)(2,1)} %fusion.22), channel_id=1, source_target_pairs={{2,0},{3,1},{4,2},{5,3},{6,4},{7,5},{8,6},{9,7},{10,8},{11,9},{12,... | collective-permute-start | bytes 3145736 | tf_op jit(solution)/shard_map/ppermute | solution.py:33
  37.8 19.5 %collective-permute-done.1 = bf16[32,64,256]{2,1,0:T(8,128)(2,1)} collective-permute-done((bf16[32,64,256]{2,1,0:T(8,128)(2,1)}, bf16[32,64,256]{2,1,0:T(8,128)(2,1)}, u32[]{:S(2)}, u32[]{:S(2)}) %collective-permute-start.1) | collective-permute-done | bytes 1048608 | tf_op jit(solution)/shard_map/ppermute | solution.py:33
  57.3 3.5 fusion.112
  60.7 2.4 collective-permute-start.2
  63.1 45.5 %collective-permute-done.2 = bf16[32,64,256]{2,1,0:T(8,128)(2,1)S(1)} collective-permute-done((bf16[32,64,256]{2,1,0:T(8,128)(2,1)}, bf16[32,64,256]{2,1,0:T(8,128)(2,1)S(1)}, u32[]{:S(2)}, u32[]{:S(2)}) %collective-permute-start.2) | collective-permute-done | bytes 1048608 | tf_op jit(solution)/shard_map/ppermute | solution.py:33
  108.6 1.3 fusion.23
  109.9 29.4 %collective-permute-done.3 = bf16[32,64,256]{2,1,0:T(8,128)(2,1)} collective-permute-done((bf16[32,64,256]{2,1,0:T(8,128)(2,1)}, bf16[32,64,256]{2,1,0:T(8,128)(2,1)}, u32[]{:S(2)}, u32[]{:S(2)}) %collective-permute-start.3) | collective-permute-done | bytes 1048608 | tf_op jit(solution)/shard_map/ppermute | solution.py:33
  139.3 2.7 fusion.34
  142.0 18.1 %collective-permute-start.4 = (bf16[32,64,256]{2,1,0:T(8,128)(2,1)}, bf16[32,64,256]{2,1,0:T(8,128)(2,1)}, u32[]{:S(2)}, u32[]{:S(2)}) collective-permute-start(bf16[32,64,256]{2,1,0:T(8,128)(2,1)} %fusion.34), channel_id=1, source_target_pairs={{16,0},{17,1},{18,2},{19,3},{20,4},{21,5},{22,6},{23,7},{24,8},{25... | collective-permute-start | bytes 3145736 | tf_op jit(solution)/shard_map/ppermute | solution.py:33
  160.7 21.5 %collective-permute-done.4 = bf16[32,64,256]{2,1,0:T(8,128)(2,1)} collective-permute-done((bf16[32,64,256]{2,1,0:T(8,128)(2,1)}, bf16[32,64,256]{2,1,0:T(8,128)(2,1)}, u32[]{:S(2)}, u32[]{:S(2)}) %collective-permute-start.4) | collective-permute-done | bytes 1048608 | tf_op jit(solution)/shard_map/ppermute | solution.py:33
  182.2 2.1 convert_select_fusion
  184.3 1.3 copy-done.2
  185.7 0.8 fusion.114
  186.5 8.5 %collective-permute-start.5 = (f32[7,64,256]{2,1,0:T(8,128)}, f32[7,64,256]{2,1,0:T(8,128)S(1)}, u32[]{:S(2)}, u32[]{:S(2)}) collective-permute-start(f32[7,64,256]{2,1,0:T(8,128)} %get-tuple-element.9), channel_id=1, source_target_pairs={{0,1},{1,2},{2,3},{3,4},{4,5},{5,6},{6,7},{7,8},{8,9},{9,10},{10,1... | collective-permute-start | bytes 1376264 | tf_op jit(solution)/shard_map/ppermute | solution.py:21
  196.6 1.2 fusion.64
  197.8 1.2 fusion.58
  199.0 1.7 collective-permute-done.5
  200.7 2.9 collective-permute-done.6
  203.6 1.9 pad_maximum_fusion
  205.5 2.9 fusion.35
  208.4 2.9 fusion.36
  211.3 3.0 fusion.8
  214.3 3.3 convert_divide_fusion
  217.6 2.8 fusion.41
  220.5 2.8 fusion.46
  223.3 3.0 fusion
  226.3 3.2 subtract_multiply_fusion
  229.5 1.3 copy-done.1
  230.8 0.9 fusion.113
  231.7 0.8 collective-permute-start.8
  232.5 4.9 collective-permute-done.7
  237.4 2.5 collective-permute-done.8
  239.9 1.9 pad_maximum_fusion.1
  242.4 23.0 %collective-permute-done.9 = f32[32,64,256]{2,1,0:T(8,128)S(1)} collective-permute-done((f32[32,64,256]{2,1,0:T(8,128)S(1)}, f32[32,64,256]{2,1,0:T(8,128)S(1)}, u32[]{:S(2)}, u32[]{:S(2)}) %collective-permute-start.9) | collective-permute-done | bytes 2097184 | tf_op jit(solution)/shard_map/ppermute | solution.py:33
  265.4 0.7 broadcast_select_fusion
  266.2 49.0 %collective-permute-done.10 = f32[32,64,256]{2,1,0:T(8,128)S(1)} collective-permute-done((f32[32,64,256]{2,1,0:T(8,128)S(1)}, f32[32,64,256]{2,1,0:T(8,128)S(1)}, u32[]{:S(2)}, u32[]{:S(2)}) %collective-permute-start.10) | collective-permute-done | bytes 2097184 | tf_op jit(solution)/shard_map/ppermute | solution.py:33
  315.6 1.4 collective-permute-start.11
  317.0 52.7 %collective-permute-done.11 = f32[32,64,256]{2,1,0:T(8,128)S(1)} collective-permute-done((f32[32,64,256]{2,1,0:T(8,128)S(1)}, f32[32,64,256]{2,1,0:T(8,128)S(1)}, u32[]{:S(2)}, u32[]{:S(2)}) %collective-permute-start.11) | collective-permute-done | bytes 2097184 | tf_op jit(solution)/shard_map/ppermute | solution.py:33
  370.0 43.5 %collective-permute-start.12 = (f32[32,64,256]{2,1,0:T(8,128)S(1)}, f32[32,64,256]{2,1,0:T(8,128)S(1)}, u32[]{:S(2)}, u32[]{:S(2)}) collective-permute-start(f32[32,64,256]{2,1,0:T(8,128)S(1)} %broadcast_select_fusion.2), channel_id=1, source_target_pairs={{24,0},{25,1},{26,2},{27,3},{28,4},{29,5},{30,6},{31,7},{0,8},{1,9... | collective-permute-start | bytes 6291464 | tf_op jit(solution)/shard_map/ppermute | solution.py:33
  413.5 44.9 %collective-permute-done.12 = f32[32,64,256]{2,1,0:T(8,128)S(1)} collective-permute-done((f32[32,64,256]{2,1,0:T(8,128)S(1)}, f32[32,64,256]{2,1,0:T(8,128)S(1)}, u32[]{:S(2)}, u32[]{:S(2)}) %collective-permute-start.12) | collective-permute-done | bytes 2097184 | tf_op jit(solution)/shard_map/ppermute | solution.py:33
  458.9 46.8 %collective-permute-done.13 = f32[32,64,256]{2,1,0:T(8,128)S(1)} collective-permute-done((f32[32,64,256]{2,1,0:T(8,128)S(1)}, f32[32,64,256]{2,1,0:T(8,128)S(1)}, u32[]{:S(2)}, u32[]{:S(2)}) %collective-permute-start.13) | collective-permute-done | bytes 2097184 | tf_op jit(solution)/shard_map/ppermute | solution.py:33
  505.6 1.7 select_log_fusion
  507.3 222.6 %all-reduce.2.cloned.1.call-done = f32[32,64,256]{2,1,0:T(8,128)} async-done(((f32[32,64,256]{2,1,0:T(8,128)}), f32[32,64,256]{2,1,0:T(8,128)}) %all-reduce.2.cloned.1.call-update) | async-done | bytes 2097168 | tf_op jit(solution)/shard_map/psum | solution.py:98
  729.9 3.4 exponential_multiply_fusion
  (23 shorter events, 3.5 us)
Async XLA Ops:
  6.5 18.6 %copy-start = (f32[32,64,256]{2,1,0:T(8,128)S(1)}, f32[32,64,256]{2,1,0:T(8,128)}, u32[]{:S(2)}) copy-start(f32[32,64,256]{2,1,0:T(8,128)} %param.5) | copy-start | bytes 6291460
  6.5 723.4 %all-reduce.2.cloned.1.call-start = ((), (), s32[]{:S(2)}) async-start(), calls=%async_computation | async-start | bytes 4194304 | tf_op jit(solution)/shard_map/psum | solution.py:98
  9.4 15.7 %collective-permute-start = (bf16[32,64,256]{2,1,0:T(8,128)(2,1)}, bf16[32,64,256]{2,1,0:T(8,128)(2,1)S(1)}, u32[]{:S(2)}, u32[]{:S(2)}) collective-permute-start(bf16[32,64,256]{2,1,0:T(8,128)(2,1)} %convert_element_type.66), channel_id=1, source_target_pairs={{1,0},{2,1},{3,2},{4,3},{5,4},{6,5},{7,6},{8,7},{9,8},{10,9},{11,1... | collective-permute-start | bytes 3145736 | tf_op jit(solution)/shard_map/ppermute | solution.py:33
  26.4 30.8 %collective-permute-start.1 = (bf16[32,64,256]{2,1,0:T(8,128)(2,1)}, bf16[32,64,256]{2,1,0:T(8,128)(2,1)}, u32[]{:S(2)}, u32[]{:S(2)}) collective-permute-start(bf16[32,64,256]{2,1,0:T(8,128)(2,1)} %fusion.22), channel_id=1, source_target_pairs={{2,0},{3,1},{4,2},{5,3},{6,4},{7,5},{8,6},{9,7},{10,8},{11,9},{12,... | collective-permute-start | bytes 3145736 | tf_op jit(solution)/shard_map/ppermute | solution.py:33
  60.7 47.8 %collective-permute-start.2 = (bf16[32,64,256]{2,1,0:T(8,128)(2,1)}, bf16[32,64,256]{2,1,0:T(8,128)(2,1)S(1)}, u32[]{:S(2)}, u32[]{:S(2)}) collective-permute-start(bf16[32,64,256]{2,1,0:T(8,128)(2,1)} %get-tuple-element.5), channel_id=1, source_target_pairs={{4,0},{5,1},{6,2},{7,3},{8,4},{9,5},{10,6},{11,7},{12,8},{13,9},{1... | collective-permute-start | bytes 3145736 | tf_op jit(solution)/shard_map/ppermute | solution.py:33
  109.9 29.4 %collective-permute-start.3 = (bf16[32,64,256]{2,1,0:T(8,128)(2,1)}, bf16[32,64,256]{2,1,0:T(8,128)(2,1)}, u32[]{:S(2)}, u32[]{:S(2)}) collective-permute-start(bf16[32,64,256]{2,1,0:T(8,128)(2,1)} %fusion.23), channel_id=1, source_target_pairs={{8,0},{9,1},{10,2},{11,3},{12,4},{13,5},{14,6},{15,7},{16,8},{17,9... | collective-permute-start | bytes 3145736 | tf_op jit(solution)/shard_map/ppermute | solution.py:33
  109.9 50.2 %copy-start.3 = (f32[1,256]{1,0:T(1,128)S(1)}, f32[1,256]{1,0:T(1,128)}, u32[]{:S(2)}) copy-start(f32[1,256]{1,0:T(1,128)} %param.7) | copy-start | bytes 3076
  142.0 40.2 %collective-permute-start.4 = (bf16[32,64,256]{2,1,0:T(8,128)(2,1)}, bf16[32,64,256]{2,1,0:T(8,128)(2,1)}, u32[]{:S(2)}, u32[]{:S(2)}) collective-permute-start(bf16[32,64,256]{2,1,0:T(8,128)(2,1)} %fusion.34), channel_id=1, source_target_pairs={{16,0},{17,1},{18,2},{19,3},{20,4},{21,5},{22,6},{23,7},{24,8},{25... | collective-permute-start | bytes 3145736 | tf_op jit(solution)/shard_map/ppermute | solution.py:33
  184.3 1.3 copy-start.2
  186.5 14.2 %collective-permute-start.5 = (f32[7,64,256]{2,1,0:T(8,128)}, f32[7,64,256]{2,1,0:T(8,128)S(1)}, u32[]{:S(2)}, u32[]{:S(2)}) collective-permute-start(f32[7,64,256]{2,1,0:T(8,128)} %get-tuple-element.9), channel_id=1, source_target_pairs={{0,1},{1,2},{2,3},{3,4},{4,5},{5,6},{6,7},{7,8},{8,9},{9,10},{10,1... | collective-permute-start | bytes 1376264 | tf_op jit(solution)/shard_map/ppermute | solution.py:21
  194.9 8.6 %collective-permute-start.6 = (f32[7,64,256]{2,1,0:T(8,128)S(1)}, f32[7,64,256]{2,1,0:T(8,128)S(1)}, u32[]{:S(2)}, u32[]{:S(2)}) collective-permute-start(f32[7,64,256]{2,1,0:T(8,128)S(1)} %get-tuple-element.10), channel_id=1, source_target_pairs={{1,0},{2,1},{3,2},{4,3},{5,4},{6,5},{7,6},{8,7},{9,8},{10,9},{11,1... | collective-permute-start | bytes 1376264 | tf_op jit(solution)/shard_map/ppermute | solution.py:23
  211.3 3.0 copy-start.4
  229.5 1.3 copy-start.1
  231.7 5.7 collective-permute-start.7
  231.7 8.2 %collective-permute-start.8 = (f32[7,64,256]{2,1,0:T(8,128)S(1)}, f32[7,64,256]{2,1,0:T(8,128)S(1)}, u32[]{:S(2)}, u32[]{:S(2)}) collective-permute-start(f32[7,64,256]{2,1,0:T(8,128)S(1)} %get-tuple-element.8), channel_id=1, source_target_pairs={{1,0},{2,1},{3,2},{4,3},{5,4},{6,5},{7,6},{8,7},{9,8},{10,9},{11,1... | collective-permute-start | bytes 1376264 | tf_op jit(solution)/shard_map/ppermute | solution.py:23
  242.3 23.1 %collective-permute-start.9 = (f32[32,64,256]{2,1,0:T(8,128)S(1)}, f32[32,64,256]{2,1,0:T(8,128)S(1)}, u32[]{:S(2)}, u32[]{:S(2)}) collective-permute-start(f32[32,64,256]{2,1,0:T(8,128)S(1)} %multiply_add_fusion), channel_id=1, source_target_pairs={{31,0},{0,1},{1,2},{2,3},{3,4},{4,5},{5,6},{6,7},{7,8},{8,9},{9,10... | collective-permute-start | bytes 6291464 | tf_op jit(solution)/shard_map/ppermute | solution.py:33
  266.1 49.1 %collective-permute-start.10 = (f32[32,64,256]{2,1,0:T(8,128)S(1)}, f32[32,64,256]{2,1,0:T(8,128)S(1)}, u32[]{:S(2)}, u32[]{:S(2)}) collective-permute-start(f32[32,64,256]{2,1,0:T(8,128)S(1)} %broadcast_select_fusion), channel_id=1, source_target_pairs={{30,0},{31,1},{0,2},{1,3},{2,4},{3,5},{4,6},{5,7},{6,8},{7,9},{8,1... | collective-permute-start | bytes 6291464 | tf_op jit(solution)/shard_map/ppermute | solution.py:33
  315.6 54.0 %collective-permute-start.11 = (f32[32,64,256]{2,1,0:T(8,128)S(1)}, f32[32,64,256]{2,1,0:T(8,128)S(1)}, u32[]{:S(2)}, u32[]{:S(2)}) collective-permute-start(f32[32,64,256]{2,1,0:T(8,128)S(1)} %broadcast_select_fusion.1), channel_id=1, source_target_pairs={{28,0},{29,1},{30,2},{31,3},{0,4},{1,5},{2,6},{3,7},{4,8},{5,9},{6... | collective-permute-start | bytes 6291464 | tf_op jit(solution)/shard_map/ppermute | solution.py:33
  370.0 88.4 %collective-permute-start.12 = (f32[32,64,256]{2,1,0:T(8,128)S(1)}, f32[32,64,256]{2,1,0:T(8,128)S(1)}, u32[]{:S(2)}, u32[]{:S(2)}) collective-permute-start(f32[32,64,256]{2,1,0:T(8,128)S(1)} %broadcast_select_fusion.2), channel_id=1, source_target_pairs={{24,0},{25,1},{26,2},{27,3},{28,4},{29,5},{30,6},{31,7},{0,8},{1,9... | collective-permute-start | bytes 6291464 | tf_op jit(solution)/shard_map/ppermute | solution.py:33
  458.8 46.9 %collective-permute-start.13 = (f32[32,64,256]{2,1,0:T(8,128)S(1)}, f32[32,64,256]{2,1,0:T(8,128)S(1)}, u32[]{:S(2)}, u32[]{:S(2)}) collective-permute-start(f32[32,64,256]{2,1,0:T(8,128)S(1)} %broadcast_select_fusion.3), channel_id=1, source_target_pairs={{16,0},{17,1},{18,2},{19,3},{20,4},{21,5},{22,6},{23,7},{24,8},{25... | collective-permute-start | bytes 6291464 | tf_op jit(solution)/shard_map/ppermute | solution.py:33
Sparse Core Ops, SparseCore 0:
  507.5 222.4 all-reduce.1
where the time goes:
time: 749 us; the launch traced here: 740 us
  waiting for transfers between devices  578 us (77%)
  starting transfers between devices  89.9 us (12%)
  matrix products  26.3 us (4%)
  other arithmetic  26.2 us (3%)
  between operations  15.2 us (2%)
    ppermute x10, waiting for transfers between devices, from_behind(): return lax.ppermute(block, axis, route)  344 us
    psum x1, waiting for transfers between devices, body(): summed = lax.psum(log_terms, 'view')  223 us
    ppermute x10, starting transfers between devices, from_behind(): return lax.ppermute(block, axis, route)  80.2 us
    dot_general x10, matrix products, matmul_high(): jnp.dot(left, right, precision=lax.Precision.HIGHEST, preferred_element_t...  26.3 us
  transfers between devices with their start and end apart: 15, of which 15 were waited for; matrix products, arithmetic and copies ran while one was open for 0% of the time, Pallas kernels for 0%

commit v1 on v0

v1 whole, which is shorter than its diff:
```python
import functools

import jax
import jax.numpy as jnp
from jax import lax
from jax.experimental import pallas as pl
from jax.experimental.pallas import tpu as pltpu
from jax.sharding import PartitionSpec as P

PROFILE_SIGMA = 48.0
CORR_MID = 2.125
CORR_SCALE = 32700.0 / 1.9
LOG_SCALE = 32700.0 / 11.2


def encode(value):
    whole = jnp.floor(jnp.clip(value, -32767.0, 32767.0) + 0.5)
    return whole.astype(jnp.int32).astype(jnp.int16)


def decode(code):
    return code.astype(jnp.int32).astype(jnp.float32)


def blur_matrix(profile):
    length = profile.shape[1]
    column = lax.broadcasted_iota(jnp.int32, (8, length), 1)
    distance = jnp.minimum(column, length - column).astype(jnp.float32)
    weights = profile * jnp.exp(-distance * distance / (2.0 * PROFILE_SIGMA * PROFILE_SIGMA))
    kernel = weights / jnp.sum(weights, axis=1, keepdims=True)
    rows = jnp.broadcast_to(kernel[:1], (length, length))
    return pltpu.roll(rows, 0, 1, stride=1, stride_axis=0)


def view_kernel(move_ref, blend_ref, profile_ref, meas_ref, est_ref, out_ref, e_ref, m_ref, b_ref):
    slabs, rows = 32, 32
    total = slabs * rows
    shift, offset = move_ref[0], move_ref[1]
    a = blend_ref[0]
    b = 1.0 - a
    skip = lax.div(8 - offset, 8)
    turn = lax.rem(40 - (8 - offset - 8 * skip), 40)
    matrix = blur_matrix(profile_ref[...]).astype(jnp.bfloat16)

    def one_line(line, carry):
        def fill(t, c):
            base = pl.multiple_of(t * rows, rows)
            for h in range(2):
                lanes = pl.ds(128 * h, 128)
                for g in range(4):
                    e_ref[pl.ds(base + 8 * g, 8), lanes] = est_ref[
                        h * 4 + g, 2 * t + line
                    ].astype(jnp.float32)
                m_ref[pl.ds(base + 8, rows), lanes] = meas_ref[
                    2 * t + line, pl.ds(32 * h, 32)
                ].astype(jnp.float32)
            return c

        lax.fori_loop(0, slabs, fill, 0)
        e_ref[pl.ds(total, 8)] = e_ref[pl.ds(0, 8)]
        m_ref[pl.ds(0, 8)] = m_ref[pl.ds(total, 8)]
        m_ref[pl.ds(total + 8, 8)] = m_ref[pl.ds(8, 8)]

        group = 4

        def blur(k, c):
            base = pl.multiple_of(k * (rows * group), rows * group)
            wide = e_ref[pl.ds(base, rows * group + 8)]
            warped = a * wide[: rows * group] + b * wide[1 : rows * group + 1]
            warped = warped.astype(jnp.bfloat16)
            forward = jnp.dot(warped, matrix, preferred_element_type=jnp.float32)
            parts = []
            for q in range(group):
                t = lax.rem(k * group + q - shift + 2 * slabs, slabs)
                start = pl.multiple_of(t * rows + 8 * skip, 8)
                wide = m_ref[pl.ds(start, rows + 8)]
                parts.append(pltpu.roll(wide, turn, 0)[:rows])
            ratios = (jnp.concatenate(parts, axis=0) / forward).astype(jnp.bfloat16)
            back = lax.dot_general(
                ratios, matrix, (((1,), (1,)), ((), ())), preferred_element_type=jnp.float32
            )
            b_ref[pl.ds(base + 8, rows * group)] = back
            return c

        lax.fori_loop(0, slabs // group, blur, 0)
        b_ref[pl.ds(0, 8)] = b_ref[pl.ds(total, 8)]

        def join(s, c):
            base = pl.multiple_of(s * rows, rows)
            wide = b_ref[pl.ds(base, rows + 8)]
            correction = a * wide[8:] + b * wide[7 : rows + 7]
            code = encode((correction - CORR_MID) * CORR_SCALE)
            for h in range(2):
                for g in range(4):
                    out_ref[h * 4 + g, 2 * s + line] = code[8 * g : 8 * g + 8, 128 * h : 128 * h + 128]
            return c

        lax.fori_loop(0, slabs, join, 0)
        return carry

    lax.fori_loop(0, 2, one_line, 0)


def final_kernel(est_ref, code_ref, out_ref):
    for h in range(2):
        lanes = pl.ds(128 * h, 128)
        factor = jnp.exp(decode(code_ref[h, 0]) * (1.0 / LOG_SCALE))
        out_ref[:, :, lanes] = est_ref[:, :, lanes] * factor


VMEM = pl.BlockSpec(memory_space=pltpu.VMEM)
SMEM = pl.BlockSpec(memory_space=pltpu.SMEM)


def body(estimate, measured, blur_profile, view_offset, tile_shift):
    views = lax.axis_size("view")
    view = lax.axis_index("view")
    blend = (view + 1).astype(jnp.float32) / (views + 1)
    group, half = view % 4, view // 4

    piece = lax.dynamic_slice(estimate, (8 * group, 0, 128 * half), (8, 64, 128))
    piece = piece.astype(jnp.bfloat16).transpose(1, 0, 2)
    image = measured[0].reshape(32, 64, 2, 128).transpose(1, 2, 0, 3).reshape(64, 64, 128)
    send = jnp.concatenate([image, piece], axis=1)
    lines = lax.all_to_all(send, "tile", 0, 0, tiled=True)

    piece = jnp.broadcast_to(lines[None, :, 64:], (8, 64, 8, 128))
    est_lines = lax.all_to_all(piece, "view", 0, 0, tiled=True)

    codes = pl.pallas_call(
        view_kernel,
        out_shape=jax.ShapeDtypeStruct((8, 64, 8, 128), jnp.int16),
        in_specs=[SMEM, SMEM, VMEM, VMEM, VMEM],
        out_specs=VMEM,
        scratch_shapes=[
            pltpu.VMEM((1032, 256), jnp.float32),
            pltpu.VMEM((1040, 256), jnp.float32),
            pltpu.VMEM((1032, 256), jnp.float32),
        ],
        name="view_kernel",
    )(
        jnp.stack([tile_shift[0], view_offset[0]]),
        blend.reshape(1),
        jnp.broadcast_to(blur_profile, (8, 256)),
        lines,
        est_lines,
    )
    codes = lax.all_to_all(codes, "view", 0, 0, tiled=True)
    product = jnp.prod(decode(codes) * (1.0 / CORR_SCALE) + CORR_MID, axis=0)
    logs = encode(jnp.log(product) * LOG_SCALE)
    logs = lax.all_to_all(logs, "tile", 0, 0, tiled=True)
    logs = jnp.broadcast_to(logs.transpose(1, 0, 2)[None], (8, 8, 64, 128))
    logs = lax.all_to_all(logs, "view", 0, 0, tiled=True)

    return pl.pallas_call(
        final_kernel,
        grid=(4,),
        out_shape=jax.ShapeDtypeStruct((32, 64, 256), jnp.float32),
        in_specs=[
            pl.BlockSpec((8, 64, 256), lambda g: (g, 0, 0)),
            pl.BlockSpec((2, 1, 8, 64, 128), lambda g: (0, g, 0, 0, 0)),
        ],
        out_specs=pl.BlockSpec((8, 64, 256), lambda g: (g, 0, 0)),
        name="final_kernel",
    )(estimate, logs.reshape(2, 4, 8, 64, 128))


def solution(mesh):
    placed = (
        P("tile", None, None),
        P("view", "tile", None, None),
        P("view", None),
        P("view"),
        P("view"),
    )
    return jax.shard_map(
        body, mesh=mesh, in_specs=placed, out_specs=P("tile", None, None), check_vma=False
    )
```

time: 749 us -> 139 us (0.19); the launches traced: 740 us -> 138 us
  waiting for transfers between devices: 578 us -> 13.9 us
  blocking collectives: 0 us -> 97.5 us
  starting transfers between devices: 89.9 us -> 4.13 us
  matrix products: 26.3 us -> 0 us
  other arithmetic: 26.2 us -> 1.33 us
  Pallas kernels: 0 us -> 14 us
  between operations: 15.2 us -> 1.36 us
    ppermute x14 -> x0, waiting for transfers between devices: 356 us -> none  [the longest x10 344 us: from_behind(): return lax.ppermute(block, axis, route)]
    psum x1 -> x0, waiting for transfers between devices: 223 us -> none  [body(): summed = lax.psum(log_terms, 'view')]
    all_to_all x0 -> x4, blocking collectives: none -> 97.5 us  [the longest x1 45.4 us: body(): lines = lax.all_to_all(send, 'tile', 0, 0, tiled=True)]
    ppermute x14 -> x0, starting transfers between devices: 89.9 us -> none  [the longest x10 80.2 us: from_behind(): return lax.ppermute(block, axis, route)]
    dot_general x10 -> x0, matrix products: 26.3 us -> none  [matmul_high(): jnp.dot(left, right, precision=lax.Precision.HIGHEST, preferred_element_t...]
    pallas_call x0 -> x2, Pallas kernels: none -> 14 us  [the longest x1 9.95 us: body(): pl.pallas_call(view_kernel, out_shape=jax.ShapeDtypeStruct((8, 64, 8, 128...]
    all_to_all x0 -> x1, waiting for transfers between devices: none -> 13.9 us  [body(): est_lines = lax.all_to_all(piece, 'view', 0, 0, tiled=True)]
    convert_element_type x5 -> x1, other arithmetic: 11.7 us -> 0.09 us  [encode(): return whole.astype(jnp.int32).astype(jnp.int16)]
  transfers between devices with their start and end apart: 15 -> 1, of which waited for: 15 -> 1; matrix products, arithmetic and copies ran while one was open for 0% -> 0% of each run, Pallas kernels for 0% -> 0%
where the time goes in v1:
time: 139 us; the launch traced here: 138 us
  blocking collectives  97.5 us (70%)
  Pallas kernels  14 us (10%)
  waiting for transfers between devices  13.9 us (10%)
  local copies, waits for them, and re-layouts  6.16 us (4%)
  starting transfers between devices  4.13 us (3%)
    all_to_all x1, blocking collectives, body(): lines = lax.all_to_all(send, 'tile', 0, 0, tiled=True)  45.4 us
    all_to_all x1, blocking collectives, body(): codes = lax.all_to_all(codes, 'view', 0, 0, tiled=True)  18.3 us
    all_to_all x1, blocking collectives, body(): logs = lax.all_to_all(logs, 'view', 0, 0, tiled=True)  17.7 us
    all_to_all x1, blocking collectives, body(): logs = lax.all_to_all(logs, 'tile', 0, 0, tiled=True)  16.1 us
    all_to_all x1, waiting for transfers between devices, body(): est_lines = lax.all_to_all(piece, 'view', 0, 0, tiled=True)  13.9 us
    pallas_call x1, Pallas kernels, body(): pl.pallas_call(view_kernel, out_shape=jax.ShapeDtypeStruct((8, 64, 8, 128...  9.95 us
    all_to_all x1, starting transfers between devices, body(): est_lines = lax.all_to_all(piece, 'view', 0, 0, tiled=True)  4.13 us
    pallas_call x1, Pallas kernels, body(): pl.pallas_call(final_kernel, grid=(4,), out_shape=jax.ShapeDtypeStruct((3...  4.08 us
  transfers between devices with their start and end apart: 1, of which 1 were waited for; matrix products, arithmetic and copies ran while one was open for 0% of the time, Pallas kernels for 0%

profile of v1, /device:TPU:1, one launch (start us, length us, event | category | flops | bytes accessed | tf_op | source)
XLA Modules:
  0.0 138.4 jit_solution(8106776743788386700)
XLA Ops:
  0.0 1.0 constant_dynamic-slice_fusion
  1.0 0.1 copy.15
  1.1 1.3 reshape_squeeze.3
  2.4 1.2 copy.8
  3.7 0.1 pad_maximum_fusion
  3.8 45.4 %all_to_all.25.meas_ref = bf16[64,72,128]{2,1,0:T(8,128)(2,1)S(1)} all-to-all(bf16[64,72,128]{2,1,0:T(8,128)(2,1)S(1)} %pad_maximum_fusion), channel_id=1, replica_groups=mesh['view'=8,'tile'=32] {'tile'}, dimensions={0} | all-to-all | bytes 2359296 | tf_op jit(solution)/shard_map/all_to_all | solution.py:125
  49.2 0.0 copy-start
  49.2 0.0 copy-start.2
  49.2 1.3 broadcast_in_dim.10
  50.5 4.1 %all-to-all-start.1 = ((bf16[8,64,8,128]{3,2,1,0:T(8,128)(2,1)}), bf16[8,64,8,128]{3,2,1,0:T(8,128)(2,1)S(1)}, u32[]{:S(2)}, u32[]{:S(2)}) async-start(bf16[8,64,8,128]{3,2,1,0:T(8,128)(2,1)} %broadcast_in_dim.10), calls=%async_computation.1 | async-start | bytes 2097152 | tf_op jit(solution)/shard_map/all_to_all | solution.py:128
  55.9 0.6 pad_add_fusion.move_ref
  56.6 13.9 %all-to-all-done.1.est_ref = bf16[8,64,8,128]{3,2,1,0:T(8,128)(2,1)S(1)} async-done(((bf16[8,64,8,128]{3,2,1,0:T(8,128)(2,1)}), bf16[8,64,8,128]{3,2,1,0:T(8,128)(2,1)S(1)}, u32[]{:S(2)}, u32[]{:S(2)}) %all-to-all-start.1) | async-done | bytes 1048608 | tf_op jit(solution)/shard_map/all_to_all | solution.py:128
  70.5 0.0 copy-start.1
  70.5 0.0 copy-done.2
  70.5 0.6 broadcast_in_dim.9.profile_ref
  71.1 0.0 copy-done
  71.1 0.3 copy-done.1
  71.5 9.9 %view_kernel.1 = s16[8,64,8,128]{3,2,1,0:T(8,128)(2,1)} custom-call(s32[2]{0:T(128)} %pad_add_fusion.move_ref, f32[1]{0:T(128)} %bitcast.blend_ref, f32[8,256]{1,0:T(8,128)} %broadcast_in_dim.9.profile_ref, bf16[64,72,128]{2,1,0:T(8,128)(2,1)} %copy-done, bf16[8,64,8,128]{3,2,1,0:T(8,128)(2,1)} %copy-done.1), custom_call_target="tpu_custom_call" | custom-call | tf_op jit(solution)/shard_map/view_kernel/pallas_call | solution.py:130
  81.4 18.3 %all_to_all.26 = s16[8,64,8,128]{3,2,1,0:T(8,128)(2,1)S(1)} all-to-all(s16[8,64,8,128]{3,2,1,0:T(8,128)(2,1)} %view_kernel.1), channel_id=1, replica_groups=mesh['view'=8,'tile'=32] {'view'}, dimensions={0} | all-to-all | bytes 2097152 | tf_op jit(solution)/shard_map/all_to_all | solution.py:148
  99.7 0.5 add_reduce_fusion
  100.2 0.1 convert_convert_fusion
  100.3 16.1 %all_to_all.27 = s16[64,8,128]{2,1,0:T(8,128)(2,1)S(1)} all-to-all(s16[64,8,128]{2,1,0:T(8,128)(2,1)S(1)} %convert_convert_fusion), channel_id=1, replica_groups=mesh['view'=8,'tile'=32] {'tile'}, dimensions={0} | all-to-all | bytes 262144 | tf_op jit(solution)/shard_map/all_to_all | solution.py:151
  116.4 0.2 broadcast_in_dim.22
  116.7 17.7 %all_to_all.28 = s16[8,8,64,128]{3,2,1,0:T(8,128)(2,1)} all-to-all(s16[8,8,64,128]{3,2,1,0:T(8,128)(2,1)S(1)} %broadcast_in_dim.22), channel_id=1, replica_groups=mesh['view'=8,'tile'=32] {'view'}, dimensions={0} | all-to-all | bytes 2097152 | tf_op jit(solution)/shard_map/all_to_all | solution.py:153
  134.3 4.1 %final_kernel.1 = f32[32,64,256]{2,1,0:T(8,128)} custom-call(f32[32,64,256]{2,1,0:T(8,128)} %est_ref.1, s16[2,4,8,64,128]{4,3,2,1,0:T(8,128)(2,1)} %bitcast.12), custom_call_target="tpu_custom_call" | custom-call | tf_op jit(solution)/shard_map/final_kernel/pallas_call | solution.py:155
  (2 shorter events, 0.0 us)
Async XLA Ops:
  49.2 21.9 %copy-start = (bf16[64,72,128]{2,1,0:T(8,128)(2,1)}, bf16[64,72,128]{2,1,0:T(8,128)(2,1)S(1)}, u32[]{:S(2)}) copy-start(bf16[64,72,128]{2,1,0:T(8,128)(2,1)S(1)} %all_to_all.25.meas_ref) | copy-start | bytes 3538948
  49.2 21.3 %copy-start.2 = (f32[1,256]{1,0:T(1,128)S(1)}, f32[1,256]{1,0:T(1,128)}, u32[]{:S(2)}) copy-start(f32[1,256]{1,0:T(1,128)} %param.7) | copy-start | bytes 3076
  50.5 20.0 %all-to-all-start.1 = ((bf16[8,64,8,128]{3,2,1,0:T(8,128)(2,1)}), bf16[8,64,8,128]{3,2,1,0:T(8,128)(2,1)S(1)}, u32[]{:S(2)}, u32[]{:S(2)}) async-start(bf16[8,64,8,128]{3,2,1,0:T(8,128)(2,1)} %broadcast_in_dim.10), calls=%async_computation.1 | async-start | bytes 2097152 | tf_op jit(solution)/shard_map/all_to_all | solution.py:128
  70.5 1.0 copy-start.1

commit v2 on v1

v2 whole, which is shorter than its diff:
```python
import jax
import jax.numpy as jnp
from jax import lax
from jax.experimental import pallas as pl
from jax.experimental.pallas import tpu as pltpu
from jax.sharding import Mesh, PartitionSpec as P

PROFILE_SIGMA = 48.0
PAIR_SCALE = 32700.0 / 2.8
TOTAL_SCALE = PAIR_SCALE / 4.0
SLABS, ROWS, LENGTH = 32, 32, 256
TOTAL = SLABS * ROWS


def blur_matrix(profile):
    column = lax.broadcasted_iota(jnp.int32, (1, LENGTH), 1)
    distance = jnp.minimum(column, LENGTH - column).astype(jnp.float32)
    weights = profile * jnp.exp(-distance * distance / (2.0 * PROFILE_SIGMA * PROFILE_SIGMA))
    kernel = weights / jnp.sum(weights, axis=1, keepdims=True)
    rows = jnp.broadcast_to(kernel, (LENGTH, LENGTH))
    return pltpu.roll(rows, 0, 1, stride=1, stride_axis=0)


def pair_kernel(
    place_ref, own_ref, other_ref, own_profile_ref, other_profile_ref, data_ref, out_ref,
    e_ref, m_ref, b_ref,
):
    upper = place_ref[0]
    column = place_ref[1]

    def fill_estimate(t, c):
        base = pl.multiple_of(t * ROWS, ROWS)
        for h in range(2):
            e_ref[pl.ds(base, ROWS), pl.ds(128 * h, 128)] = data_ref[
                h * SLABS + t, pl.ds(64, ROWS)
            ].astype(jnp.float32)
        return c

    lax.fori_loop(0, SLABS, fill_estimate, 0)
    e_ref[pl.ds(TOTAL, 8)] = e_ref[pl.ds(0, 8)]
    group = 4
    row = lax.broadcasted_iota(jnp.int32, (1, 8, LENGTH), 1)

    blends = []
    for w in range(2):
        is_own = upper == w
        shift = jnp.where(is_own, own_ref[0], other_ref[0])
        offset = jnp.where(is_own, own_ref[1], other_ref[1])
        a = (w * 4 + column + 1).astype(jnp.float32) / 9.0
        b = 1.0 - a
        blends.append((a, b))
        skip = lax.div(8 - offset, 8)
        rest = 8 - offset - 8 * skip
        turn = lax.rem(8 - rest, 8)
        profile = jnp.where(is_own, own_profile_ref[...], other_profile_ref[...])
        matrix = blur_matrix(profile).astype(jnp.bfloat16)

        def fill_image(t, c, w=w):
            base = pl.multiple_of(t * ROWS, ROWS)
            for h in range(2):
                m_ref[pl.ds(base + 8, ROWS), pl.ds(128 * h, 128)] = data_ref[
                    w * SLABS + t, pl.ds(32 * h, ROWS)
                ].astype(jnp.float32)
            return c

        lax.fori_loop(0, SLABS, fill_image, 0)
        m_ref[pl.ds(0, 8)] = m_ref[pl.ds(TOTAL, 8)]
        m_ref[pl.ds(TOTAL + 8, 8)] = m_ref[pl.ds(8, 8)]

        def blur(k, c, w=w, a=a, b=b, matrix=matrix, skip=skip, rest=rest, turn=turn, shift=shift):
            base = pl.multiple_of(k * (ROWS * group), ROWS * group)
            wide = e_ref[pl.ds(base, ROWS * group + 8)]
            warped = a * wide[: ROWS * group] + b * wide[1 : ROWS * group + 1]
            warped = warped.astype(jnp.bfloat16)
            forward = jnp.dot(warped, matrix, preferred_element_type=jnp.float32)
            parts = []
            for q in range(group):
                t = lax.rem(k * group + q - shift + 2 * SLABS, SLABS)
                start = pl.multiple_of(t * ROWS + 8 * skip, 8)
                tiles = m_ref[pl.ds(start, ROWS + 8)].reshape(5, 8, LENGTH)
                tiles = pltpu.roll(tiles, turn, 1)
                part = jnp.where(row < 8 - rest, tiles[:4], tiles[1:])
                parts.append(part.reshape(ROWS, LENGTH))
            ratios = (jnp.concatenate(parts, axis=0) / forward).astype(jnp.bfloat16)
            back = lax.dot_general(
                ratios, matrix, (((1,), (1,)), ((), ())), preferred_element_type=jnp.float32
            )
            b_ref[w, pl.ds(base + 8, ROWS * group)] = back
            return c

        lax.fori_loop(0, SLABS // group, blur, 0)
        b_ref[w, pl.ds(0, 8)] = b_ref[w, pl.ds(TOTAL, 8)]

    def join(s, c):
        base = pl.multiple_of(s * ROWS, ROWS)
        product = None
        for w, (a, b) in enumerate(blends):
            wide = b_ref[w, pl.ds(base, ROWS + 8)]
            correction = a * wide[8:] + b * wide[7 : ROWS + 7]
            product = correction if product is None else product * correction
        code = jnp.clip(jnp.log(product) * PAIR_SCALE, -32767.0, 32767.0)
        code = jnp.floor(code + 0.5).astype(jnp.int32).astype(jnp.int16)
        for g in range(4):
            out_ref[g, s] = code[8 * g : 8 * g + 8]
        return c

    lax.fori_loop(0, SLABS, join, 0)


def final_kernel(est_ref, code_ref, out_ref):
    for h in range(2):
        lines = pl.ds(32 * h, 32)
        logs = code_ref[h, 0].astype(jnp.int32).astype(jnp.float32) * (1.0 / TOTAL_SCALE)
        out_ref[:, lines] = est_ref[:, lines] * jnp.exp(logs)


VMEM = pl.BlockSpec(memory_space=pltpu.VMEM)
SMEM = pl.BlockSpec(memory_space=pltpu.SMEM)


def body(estimate, measured, blur_profile, view_offset, tile_shift):
    upper = lax.axis_index("upper")
    column = lax.axis_index("column")
    swap = [(0, 1), (1, 0)]
    moves = jnp.concatenate([tile_shift, view_offset])
    other_moves = lax.ppermute(moves, "upper", swap)
    other_profile = lax.ppermute(blur_profile, "upper", swap)

    piece = lax.dynamic_slice(estimate, (0, 0, 128 * upper), (32, 64, 128))
    piece = piece.astype(jnp.bfloat16).transpose(1, 0, 2)
    image = measured[0].reshape(32, 64, 2, 128).transpose(1, 2, 0, 3).reshape(64, 64, 128)
    send = jnp.concatenate([image, piece], axis=1)
    data = lax.all_to_all(send, ("upper", "tile"), 0, 0, tiled=True)

    codes = pl.pallas_call(
        pair_kernel,
        out_shape=jax.ShapeDtypeStruct((4, SLABS, 8, LENGTH), jnp.int16),
        in_specs=[SMEM, SMEM, SMEM, VMEM, VMEM, VMEM],
        out_specs=VMEM,
        scratch_shapes=[
            pltpu.VMEM((TOTAL + 8, LENGTH), jnp.float32),
            pltpu.VMEM((TOTAL + 16, LENGTH), jnp.float32),
            pltpu.VMEM((2, TOTAL + 8, LENGTH), jnp.float32),
        ],
        name="pair_kernel",
    )(
        jnp.stack([upper, column]),
        moves,
        other_moves,
        blur_profile,
        other_profile,
        data,
    )
    codes = lax.all_to_all(codes, "column", 0, 0, tiled=True)
    total = jnp.sum(codes.astype(jnp.int32), axis=0)
    logs = ((total + 2) >> 2).astype(jnp.int16)
    logs = lax.all_to_all(logs, "tile", 0, 0, tiled=True)
    logs = jnp.broadcast_to(logs.transpose(1, 0, 2)[None], (8, 8, 32, LENGTH))
    logs = lax.all_to_all(logs, ("upper", "column"), 0, 0, tiled=True)

    return pl.pallas_call(
        final_kernel,
        grid=(4,),
        out_shape=jax.ShapeDtypeStruct((32, 64, LENGTH), jnp.float32),
        in_specs=[
            pl.BlockSpec((8, 64, LENGTH), lambda g: (g, 0, 0)),
            pl.BlockSpec((2, 1, 8, 32, LENGTH), lambda g: (0, g, 0, 0, 0)),
        ],
        out_specs=pl.BlockSpec((8, 64, LENGTH), lambda g: (g, 0, 0)),
        name="final_kernel",
    )(estimate, logs.reshape(2, 4, 8, 32, LENGTH))


def solution(mesh):
    fine = Mesh(mesh.devices.reshape(2, 4, 32), ("upper", "column", "tile"))
    view = ("upper", "column")
    placed = (P("tile"), P(view, "tile"), P(view), P(view), P(view))
    return jax.shard_map(
        body, mesh=fine, in_specs=placed, out_specs=P("tile"), check_vma=False
    )
```

time: 139 us -> 120 us (0.86)
  blocking collectives: 97.5 us -> 46.9 us
  waiting for transfers between devices: 13.9 us -> 36.2 us
  starting transfers between devices: 4.13 us -> 14.9 us
  local copies, waits for them, and re-layouts: 6.16 us -> 4.54 us
    all_to_all x3 -> x2, blocking collectives: 81.4 us -> 31.4 us  [the longest x1 17.7 us: body(): logs = lax.all_to_all(logs, ('upper', 'column'), 0, 0, tiled=True)]
    all_to_all x1, waiting for transfers between devices: 13.9 us -> 34.2 us  [body(): data = lax.all_to_all(send, ('upper', 'tile'), 0, 0, tiled=True)]
    all_to_all x1, starting transfers between devices: 4.13 us -> 13.3 us  [body(): data = lax.all_to_all(send, ('upper', 'tile'), 0, 0, tiled=True)]
    broadcast_in_dim x3 -> x1, local copies, waits for them, and re-layouts: 2.15 us -> 0.12 us  [body(): logs = jnp.broadcast_to(logs.transpose(1, 0, 2)[None], (8, 8, 32, LENGTH))]
    ppermute x0 -> x2, waiting for transfers between devices: none -> 2 us  [the longest x1 1.13 us: body(): other_profile = lax.ppermute(blur_profile, 'upper', swap)]
    ppermute x0 -> x2, starting transfers between devices: none -> 1.6 us  [the longest x1 1.49 us: body(): other_moves = lax.ppermute(moves, 'upper', swap)]
  transfers between devices with their start and end apart: 1 -> 3, of which waited for: 1 -> 3; matrix products, arithmetic and copies ran while one was open for 0% -> 1% of each run, Pallas kernels for 0% -> 0%
where the time goes in v2:
time: 120 us; the launch traced here: 119 us
  blocking collectives  46.9 us (39%)
  waiting for transfers between devices  36.2 us (30%)
  starting transfers between devices  14.9 us (12%)
  Pallas kernels  13.4 us (11%)
  local copies, waits for them, and re-layouts  4.54 us (4%)
  other arithmetic  2.1 us (2%)
  between operations  1.38 us (1%)
    all_to_all x1, waiting for transfers between devices, body(): data = lax.all_to_all(send, ('upper', 'tile'), 0, 0, tiled=True)  34.2 us
    all_to_all x1, blocking collectives, body(): logs = lax.all_to_all(logs, ('upper', 'column'), 0, 0, tiled=True)  17.7 us
    all_to_all x1, blocking collectives, body(): logs = lax.all_to_all(logs, 'tile', 0, 0, tiled=True)  15.5 us
    all_to_all x1, blocking collectives, body(): codes = lax.all_to_all(codes, 'column', 0, 0, tiled=True)  13.8 us
    all_to_all x1, starting transfers between devices, body(): data = lax.all_to_all(send, ('upper', 'tile'), 0, 0, tiled=True)  13.3 us
    pallas_call x1, Pallas kernels, body(): pl.pallas_call(pair_kernel, out_shape=jax.ShapeDtypeStruct((4, SLABS, 8,...  9.28 us
    pallas_call x1, Pallas kernels, body(): pl.pallas_call(final_kernel, grid=(4,), out_shape=jax.ShapeDtypeStruct((3...  4.08 us
  transfers between devices with their start and end apart: 3, of which 3 were waited for; matrix products, arithmetic and copies ran while one was open for 1% of the time, Pallas kernels for 0%

profile of v2, /device:TPU:1, one launch (start us, length us, event | category | flops | bytes accessed | tf_op | source)
XLA Modules:
  0.0 119.4 jit_solution(18076796747841505690)
XLA Ops:
  0.0 0.0 copy-start.1
  0.0 1.4 %constant_dynamic-slice_fusion = bf16[32,64,128]{2,1,0:T(8,128)(2,1)S(1)} fusion(f32[32,64,256]{2,1,0:T(8,128)} %est_ref.1, s32[]{:T(128)S(6)} %select_n.3), kind=kLoop, calls=%fused_computation.7 | loop fusion | bytes 1048580 | tf_op jit(solution)/shard_map/dynamic_slice | solution.py:129
  1.4 0.3 copy.15
  1.8 0.0 copy-done.1
  1.8 0.3 reshape_squeeze.3
  2.1 1.2 %copy.8 = bf16[32,64,2,128]{3,0,2,1:T(8,128)(2,1)S(1)} copy(bf16[32,64,2,128]{3,2,1,0:T(2,128)(2,1)S(1)} %reshape_squeeze.3) | data formatting | bytes 2097152 | tf_op jit(solution)/shard_map/reshape;squeeze | solution.py:131
  3.3 1.2 %pad_maximum_fusion = bf16[64,96,128]{2,1,0:T(8,128)(2,1)} fusion(bf16[64,32,128]{2,1,0:T(8,128)(2,1)S(1)} %bitcast.14, bf16[64,64,128]{2,1,0:T(8,128)(2,1)S(1)} %bitcast.12), kind=kLoop, calls=%fused_computation | loop fusion | flops 3145728 | bytes 3145728 | tf_op jit(solution)/shard_map/concatenate | solution.py:132
  4.5 0.0 copy-start.2
  4.5 13.3 %all-to-all-start = ((bf16[64,96,128]{2,1,0:T(8,128)(2,1)}), bf16[64,96,128]{2,1,0:T(8,128)(2,1)S(1)}, u32[]{:S(2)}, u32[]{:S(2)}) async-start(bf16[64,96,128]{2,1,0:T(8,128)(2,1)} %pad_maximum_fusion), calls=%async_computation | async-start | bytes 3145728 | tf_op jit(solution)/shard_map/all_to_all | solution.py:133
  19.1 0.1 pad_add_fusion.1.own_ref
  19.2 0.0 copy-start.4
  19.2 1.5 %collective-permute-start = (s32[2]{0:T(128)S(1)}, s32[2]{0:T(128)S(1)}, u32[]{:S(2)}, u32[]{:S(2)}) collective-permute-start(s32[2]{0:T(128)S(1)} %pad_add_fusion.1.own_ref), channel_id=1, source_target_pairs={{0,128},{128,0},{1,129},{129,1},{2,130},{130,2},{3,131},{131,3},{4... | collective-permute-start | bytes 32 | tf_op jit(solution)/shard_map/ppermute | solution.py:126
  20.7 0.0 copy-done.2
  20.7 0.1 collective-permute-start.1
  20.8 0.6 pad_add_fusion.place_ref
  21.4 0.9 collective-permute-done.other_ref
  22.3 0.0 copy-start.5
  22.3 1.1 collective-permute-done.1.other_profile_ref
  23.4 0.0 copy-start.3
  23.4 34.2 %all-to-all-done.data_ref = bf16[64,96,128]{2,1,0:T(8,128)(2,1)S(1)} async-done(((bf16[64,96,128]{2,1,0:T(8,128)(2,1)}), bf16[64,96,128]{2,1,0:T(8,128)(2,1)S(1)}, u32[]{:S(2)}, u32[]{:S(2)}) %all-to-all-start) | async-done | bytes 1572896 | tf_op jit(solution)/shard_map/all_to_all | solution.py:133
  57.6 0.0 copy-done.4
  57.6 0.0 copy-done.5
  57.6 0.0 copy-done.3
  57.6 0.0 copy-start
  57.6 1.1 copy-done
  58.7 9.3 %pair_kernel.1 = s16[4,32,8,256]{3,2,1,0:T(8,128)(2,1)} custom-call(s32[2]{0:T(128)} %pad_add_fusion.place_ref, s32[2]{0:T(128)} %copy-done.4, s32[2]{0:T(128)} %copy-done.5, f32[1,256]{1,0:T(1,128)} %own_profile_ref.1, f32[1,256]{1,0:T(1,128)} %copy-done.3, bf16[64,96,128]{2,1,0:T(8,128)(2,1)} %copy-done), custom_call_target="tpu_custom_call" | custom-call | tf_op jit(solution)/shard_map/pair_kernel/pallas_call | solution.py:135
  68.0 13.8 %all_to_all.20 = s16[4,32,8,256]{3,2,1,0:T(8,128)(2,1)S(1)} all-to-all(s16[4,32,8,256]{3,2,1,0:T(8,128)(2,1)} %pair_kernel.1), channel_id=1, replica_groups=mesh['upper'=2,'column'=4,'tile'=32] {'column'}, dimensions={0} | all-to-all | bytes 1048576 | tf_op jit(solution)/shard_map/all_to_all | solution.py:154
  81.8 0.1 convert_reduce_fusion
  81.9 15.5 %all_to_all.21 = s16[32,8,256]{2,1,0:T(8,128)(2,1)S(1)} all-to-all(s16[32,8,256]{2,1,0:T(8,128)(2,1)S(1)} %shift-right-arithmetic_convert_fusion), channel_id=1, replica_groups=mesh['upper'=2,'column'=4,'tile'=32] {'tile'}, dimensions={0} | all-to-all | bytes 262144 | tf_op jit(solution)/shard_map/all_to_all | solution.py:157
  97.5 0.1 broadcast_in_dim.2
  97.6 17.7 %all_to_all.22 = s16[8,8,32,256]{3,2,1,0:T(8,128)(2,1)} all-to-all(s16[8,8,32,256]{3,2,1,0:T(8,128)(2,1)S(1)} %broadcast_in_dim.2), channel_id=1, replica_groups=mesh['upper'=2,'column'=4,'tile'=32] {'upper','column'}, dimensions={0} | all-to-all | bytes 2097152 | tf_op jit(solution)/shard_map/all_to_all | solution.py:159
  115.3 4.1 %final_kernel.1 = f32[32,64,256]{2,1,0:T(8,128)} custom-call(f32[32,64,256]{2,1,0:T(8,128)} %est_ref.1, s16[2,4,8,32,256]{4,3,2,1,0:T(8,128)(2,1)} %bitcast.13), custom_call_target="tpu_custom_call" | custom-call | tf_op jit(solution)/shard_map/final_kernel/pallas_call | solution.py:161
  (2 shorter events, 0.0 us)
Async XLA Ops:
  0.0 1.8 %copy-start.1 = (bf16[1,32,64,256]{3,2,1,0:T(8,128)(2,1)S(1)}, bf16[1,32,64,256]{3,2,1,0:T(8,128)(2,1)}, u32[]{:S(2)}) copy-start(bf16[1,32,64,256]{3,2,1,0:T(8,128)(2,1)} %param.6) | copy-start | bytes 3145732
  4.5 16.2 %copy-start.2 = (f32[1,256]{1,0:T(1,128)S(1)}, f32[1,256]{1,0:T(1,128)}, u32[]{:S(2)}) copy-start(f32[1,256]{1,0:T(1,128)} %own_profile_ref.1) | copy-start | bytes 3076
  4.5 53.0 %all-to-all-start = ((bf16[64,96,128]{2,1,0:T(8,128)(2,1)}), bf16[64,96,128]{2,1,0:T(8,128)(2,1)S(1)}, u32[]{:S(2)}, u32[]{:S(2)}) async-start(bf16[64,96,128]{2,1,0:T(8,128)(2,1)} %pad_maximum_fusion), calls=%async_computation | async-start | bytes 3145728 | tf_op jit(solution)/shard_map/all_to_all | solution.py:133
  19.2 38.4 %copy-start.4 = (s32[2]{0:T(128)}, s32[2]{0:T(128)S(1)}, u32[]{:S(2)}) copy-start(s32[2]{0:T(128)S(1)} %pad_add_fusion.1.own_ref) | copy-start | bytes 28
  19.2 3.1 %collective-permute-start = (s32[2]{0:T(128)S(1)}, s32[2]{0:T(128)S(1)}, u32[]{:S(2)}, u32[]{:S(2)}) collective-permute-start(s32[2]{0:T(128)S(1)} %pad_add_fusion.1.own_ref), channel_id=1, source_target_pairs={{0,128},{128,0},{1,129},{129,1},{2,130},{130,2},{3,131},{131,3},{4... | collective-permute-start | bytes 32 | tf_op jit(solution)/shard_map/ppermute | solution.py:126
  20.7 2.7 %collective-permute-start.1 = (f32[1,256]{1,0:T(1,128)S(1)}, f32[1,256]{1,0:T(1,128)S(1)}, u32[]{:S(2)}, u32[]{:S(2)}) collective-permute-start(f32[1,256]{1,0:T(1,128)S(1)} %copy-done.2), channel_id=1, source_target_pairs={{0,128},{128,0},{1,129},{129,1},{2,130},{130,2},{3,131},{131,3},{4... | collective-permute-start | bytes 3080 | tf_op jit(solution)/shard_map/ppermute | solution.py:127
  22.3 35.3 %copy-start.5 = (s32[2]{0:T(128)}, s32[2]{0:T(128)S(1)}, u32[]{:S(2)}) copy-start(s32[2]{0:T(128)S(1)} %collective-permute-done.other_ref) | copy-start | bytes 28
  23.4 34.2 %copy-start.3 = (f32[1,256]{1,0:T(1,128)}, f32[1,256]{1,0:T(1,128)S(1)}, u32[]{:S(2)}) copy-start(f32[1,256]{1,0:T(1,128)S(1)} %collective-permute-done.1.other_profile_ref) | copy-start | bytes 3076
  57.6 1.1 copy-start

commit v3 on v2

v3 whole, which is shorter than its diff:
```python
import jax
import jax.numpy as jnp
from jax import lax
from jax.experimental import pallas as pl
from jax.experimental.pallas import tpu as pltpu
from jax.sharding import Mesh, PartitionSpec as P

PROFILE_SIGMA = 48.0
PAIR_SCALE = 32700.0 / 2.8
TOTAL_SCALE = PAIR_SCALE / 4.0
SLABS, ROWS, LENGTH = 32, 32, 256
TOTAL = SLABS * ROWS
GROUP = 4


def blur_matrix(profile):
    column = lax.broadcasted_iota(jnp.int32, (1, LENGTH), 1)
    distance = jnp.minimum(column, LENGTH - column).astype(jnp.float32)
    weights = profile * jnp.exp(-distance * distance / (2.0 * PROFILE_SIGMA * PROFILE_SIGMA))
    kernel = weights / jnp.sum(weights, axis=1, keepdims=True)
    rows = jnp.broadcast_to(kernel, (LENGTH, LENGTH))
    return pltpu.roll(rows, 0, 1, stride=1, stride_axis=0)


def tile_rows(wide, rest, turn, row):
    tiles = pltpu.roll(wide.reshape(-1, 8, LENGTH), turn, 1)
    count = tiles.shape[0]
    tiles = jnp.where(row < 8 - rest, tiles[: count - 1], tiles[1:])
    return tiles.reshape(8 * count - 8, LENGTH)


def blend_of(column, w):
    a = (w * 4 + column + 1).astype(jnp.float32) / 9.0
    return a, 1.0 - a


def forward_kernel(
    place_ref, own_ref, other_ref, own_profile_ref, other_profile_ref, est0_ref, est1_ref,
    est2_ref, est3_ref, inverse_ref, matrix_ref, e_ref,
):
    est_refs = (est0_ref, est1_ref, est2_ref, est3_ref)
    upper, column = place_ref[0], place_ref[1]

    def fill(t, c):
        for d, est_ref in enumerate(est_refs):
            first = t * ROWS + 8 * lax.rem(column + 4 - d, 4) + 8
            e_ref[pl.ds(pl.multiple_of(first, 8), 8)] = est_ref[t].astype(jnp.float32)
        return c

    lax.fori_loop(0, SLABS, fill, 0)
    e_ref[pl.ds(0, 8)] = e_ref[pl.ds(TOTAL, 8)]
    e_ref[pl.ds(TOTAL + 8, 16)] = e_ref[pl.ds(8, 16)]
    row = lax.broadcasted_iota(jnp.int32, (1, 8, LENGTH), 1)

    for w in range(2):
        is_own = upper == w
        shift = jnp.where(is_own, own_ref[0], other_ref[0])
        offset = jnp.where(is_own, own_ref[1], other_ref[1])
        a, b = blend_of(column, w)
        skip = lax.div(8 + offset, 8)
        rest = 8 + offset - 8 * skip
        turn = lax.rem(8 - rest, 8)
        profile = jnp.where(is_own, own_profile_ref[...], other_profile_ref[...])
        matrix = blur_matrix(profile).astype(jnp.bfloat16)
        matrix_ref[w] = matrix

        def blur(k, c, w=w, a=a, b=b, matrix=matrix, skip=skip, rest=rest, turn=turn, shift=shift):
            base = pl.multiple_of(k * (ROWS * GROUP), ROWS * GROUP)
            parts = []
            for q in range(GROUP):
                s = lax.rem(k * GROUP + q + shift, SLABS)
                start = pl.multiple_of(s * ROWS + 8 * skip, 8)
                wide = tile_rows(e_ref[pl.ds(start, ROWS + 16)], rest, turn, row)
                parts.append(a * wide[:ROWS] + b * wide[1 : ROWS + 1])
            warped = jnp.concatenate(parts, axis=0).astype(jnp.bfloat16)
            forward = jnp.dot(warped, matrix, preferred_element_type=jnp.float32)
            inverse_ref[w, pl.ds(base, ROWS * GROUP)] = 1.0 / forward
            return c

        lax.fori_loop(0, SLABS // GROUP, blur, 0)


def back_kernel(
    place_ref, own_ref, other_ref, image_ref, inverse_ref, matrix_ref, out_ref, b_ref
):
    upper, column = place_ref[0], place_ref[1]
    row = lax.broadcasted_iota(jnp.int32, (1, 8, LENGTH), 1)

    for w in range(2):

        def blur(k, c, w=w):
            base = pl.multiple_of(k * (ROWS * GROUP), ROWS * GROUP)
            image = image_ref[pl.ds(w * SLABS + k * GROUP, GROUP)].reshape(ROWS * GROUP, LENGTH)
            ratios = image.astype(jnp.float32) * inverse_ref[w, pl.ds(base, ROWS * GROUP)]
            b_ref[w, pl.ds(base + 16, ROWS * GROUP)] = lax.dot_general(
                ratios.astype(jnp.bfloat16),
                matrix_ref[w],
                (((1,), (1,)), ((), ())),
                preferred_element_type=jnp.float32,
            )
            return c

        lax.fori_loop(0, SLABS // GROUP, blur, 0)
        b_ref[w, pl.ds(0, 16)] = b_ref[w, pl.ds(TOTAL, 16)]
        b_ref[w, pl.ds(TOTAL + 16, 8)] = b_ref[w, pl.ds(16, 8)]

    views = []
    for w in range(2):
        is_own = upper == w
        shift = jnp.where(is_own, own_ref[0], other_ref[0])
        offset = jnp.where(is_own, own_ref[1], other_ref[1])
        skip = lax.div(8 - offset, 8)
        rest = 8 - offset - 8 * skip
        views.append((shift, skip, rest, lax.rem(8 - rest, 8), *blend_of(column, w)))

    def join(s, c):
        product = None
        for w, (shift, skip, rest, turn, a, b) in enumerate(views):
            t = lax.rem(s - shift + SLABS, SLABS)
            start = pl.multiple_of(t * ROWS + 8 * skip, 8)
            wide = b_ref[w, pl.ds(start, ROWS + 16)]
            blended = a * wide[8:] + b * wide[7 : ROWS + 15]
            correction = tile_rows(blended, rest, turn, row)
            product = correction if product is None else product * correction
        code = jnp.clip(jnp.log(product) * PAIR_SCALE, -32767.0, 32767.0)
        code = jnp.floor(code + 0.5).astype(jnp.int32).astype(jnp.int16)
        for g in range(4):
            out_ref[g, s] = code[8 * g : 8 * g + 8]
        return c

    lax.fori_loop(0, SLABS, join, 0)


def final_kernel(est_ref, code_ref, out_ref):
    for h in range(2):
        lines = pl.ds(32 * h, 32)
        logs = code_ref[h, 0].astype(jnp.int32).astype(jnp.float32) * (1.0 / TOTAL_SCALE)
        out_ref[:, lines] = est_ref[:, lines] * jnp.exp(logs)


VMEM = pl.BlockSpec(memory_space=pltpu.VMEM)
SMEM = pl.BlockSpec(memory_space=pltpu.SMEM)


def body(estimate, measured, blur_profile, view_offset, tile_shift):
    upper = lax.axis_index("upper")
    column = lax.axis_index("column")
    swap = [(0, 1), (1, 0)]
    moves = jnp.concatenate([tile_shift, view_offset])
    other_moves = lax.ppermute(moves, "upper", swap)
    other_profile = lax.ppermute(blur_profile, "upper", swap)

    piece = lax.dynamic_slice(estimate, (8 * column, 32 * upper, 0), (8, 32, LENGTH))
    piece = piece.astype(jnp.bfloat16).transpose(1, 0, 2)
    piece = lax.all_to_all(piece, "tile", 0, 0, tiled=True)
    image = measured[0].transpose(1, 0, 2)
    image_lines = lax.all_to_all(image, ("upper", "tile"), 0, 0, tiled=True)
    est_lines = [piece]
    for d in (1, 2, 3):
        route = [(i, (i + d) % 4) for i in range(4)]
        est_lines.append(lax.ppermute(piece, "column", route))

    place = jnp.stack([upper, column])
    inverse, matrices = pl.pallas_call(
        forward_kernel,
        out_shape=(
            jax.ShapeDtypeStruct((2, TOTAL, LENGTH), jnp.float32),
            jax.ShapeDtypeStruct((2, LENGTH, LENGTH), jnp.bfloat16),
        ),
        in_specs=[SMEM] * 3 + [VMEM] * 6,
        out_specs=(VMEM, VMEM),
        scratch_shapes=[pltpu.VMEM((TOTAL + 24, LENGTH), jnp.float32)],
        cost_estimate=pl.CostEstimate(
            flops=4 * TOTAL * LENGTH * LENGTH, bytes_accessed=8 << 20, transcendentals=0
        ),
        compiler_params=pltpu.CompilerParams(vmem_limit_bytes=16 << 20),
        name="forward_kernel",
    )(place, moves, other_moves, blur_profile, other_profile, *est_lines)
    codes = pl.pallas_call(
        back_kernel,
        out_shape=jax.ShapeDtypeStruct((4, SLABS, 8, LENGTH), jnp.int16),
        in_specs=[SMEM, SMEM, SMEM, VMEM, VMEM, VMEM],
        out_specs=VMEM,
        scratch_shapes=[pltpu.VMEM((2, TOTAL + 24, LENGTH), jnp.float32)],
        compiler_params=pltpu.CompilerParams(vmem_limit_bytes=16 << 20),
        name="back_kernel",
    )(place, moves, other_moves, image_lines, inverse, matrices)
    codes = lax.all_to_all(codes, "column", 0, 0, tiled=True)
    total = jnp.sum(codes.astype(jnp.int32), axis=0)
    logs = ((total + 2) >> 2).astype(jnp.int16)
    logs = lax.all_to_all(logs, "tile", 0, 0, tiled=True)
    logs = jnp.broadcast_to(logs.transpose(1, 0, 2)[None], (8, 8, 32, LENGTH))
    logs = lax.all_to_all(logs, ("upper", "column"), 0, 0, tiled=True)

    return pl.pallas_call(
        final_kernel,
        grid=(4,),
        out_shape=jax.ShapeDtypeStruct((32, 64, LENGTH), jnp.float32),
        in_specs=[
            pl.BlockSpec((8, 64, LENGTH), lambda g: (g, 0, 0)),
            pl.BlockSpec((2, 1, 8, 32, LENGTH), lambda g: (0, g, 0, 0, 0)),
        ],
        out_specs=pl.BlockSpec((8, 64, LENGTH), lambda g: (g, 0, 0)),
        compiler_params=pltpu.CompilerParams(vmem_limit_bytes=16 << 20),
        name="final_kernel",
    )(estimate, logs.reshape(2, 4, 8, 32, LENGTH))


def solution(mesh):
    fine = Mesh(mesh.devices.reshape(2, 4, 32), ("upper", "column", "tile"))
    view = ("upper", "column")
    placed = (P("tile"), P(view, "tile"), P(view), P(view), P(view))
    return jax.shard_map(
        body, mesh=fine, in_specs=placed, out_specs=P("tile"), check_vma=False
    )
```

time: 120 us -> 114 us (0.950)
  waiting for transfers between devices: 36.2 us -> 25 us
  starting transfers between devices: 14.9 us -> 23.9 us
  other arithmetic: 2.1 us -> 0.31 us
  Pallas kernels: 13.4 us -> 11.7 us
    all_to_all x1 -> x2, waiting for transfers between devices: 34.2 us -> 18.3 us  [the longest x1 10.6 us: body(): image_lines = lax.all_to_all(image, ('upper', 'tile'), 0, 0, tiled=True)]
    all_to_all x1 -> x2, starting transfers between devices: 13.3 us -> 18.5 us  [the longest x1 12.7 us: body(): piece = lax.all_to_all(piece, 'tile', 0, 0, tiled=True)]
    ppermute x0 -> x3, waiting for transfers between devices: none -> 4.16 us  [body(): est_lines.append(lax.ppermute(piece, 'column', route))]
    ppermute x0 -> x3, starting transfers between devices: none -> 3.68 us  [body(): est_lines.append(lax.ppermute(piece, 'column', route))]
    pallas_call x1, Pallas kernels: 4.08 us -> 2.05 us  [body(): pl.pallas_call(final_kernel, grid=(4,), out_shape=jax.ShapeDtypeStruct((3...]
    unnamed x13 -> x6, local copies, waits for them, and re-layouts: 1.5 us -> 3.52 us
    another operation x2 -> x0, local copies, waits for them, and re-layouts: 1.51 us -> none  [body(): measured[0].reshape(32, 64, 2, 128).transpose(1, 2, 0, 3)]
    concatenate x1 -> x0, other arithmetic: 1.25 us -> none  [body(): send = jnp.concatenate([image, piece], axis=1)]
  transfers between devices with their start and end apart: 3 -> 7, of which waited for: 3 -> 6; matrix products, arithmetic and copies ran while one was open for 1% -> 3% of each run, Pallas kernels for 0% -> 4%
where the time goes in v3:
time: 114 us
  blocking collectives  46.8 us (41%)
  waiting for transfers between devices  25 us (22%)
  starting transfers between devices  23.9 us (21%)
  Pallas kernels  11.7 us (10%)
  local copies, waits for them, and re-layouts  4.62 us (4%)
  between operations  1.37 us (1%)
    all_to_all x1, blocking collectives, body(): logs = lax.all_to_all(logs, ('upper', 'column'), 0, 0, tiled=True)  17.3 us
    all_to_all x1, blocking collectives, body(): logs = lax.all_to_all(logs, 'tile', 0, 0, tiled=True)  16.5 us
    all_to_all x1, blocking collectives, body(): codes = lax.all_to_all(codes, 'column', 0, 0, tiled=True)  12.9 us
    all_to_all x1, starting transfers between devices, body(): piece = lax.all_to_all(piece, 'tile', 0, 0, tiled=True)  12.7 us
    all_to_all x1, waiting for transfers between devices, body(): image_lines = lax.all_to_all(image, ('upper', 'tile'), 0, 0, tiled=True)  10.6 us
    all_to_all x1, waiting for transfers between devices, body(): piece = lax.all_to_all(piece, 'tile', 0, 0, tiled=True)  7.7 us
    all_to_all x1, starting transfers between devices, body(): image_lines = lax.all_to_all(image, ('upper', 'tile'), 0, 0, tiled=True)  5.76 us
    pallas_call x1, Pallas kernels, body(): pl.pallas_call(back_kernel, out_shape=jax.ShapeDtypeStruct((4, SLABS, 8,...  5.23 us
  transfers between devices with their start and end apart: 7, of which 6 were waited for; matrix products, arithmetic and copies ran while one was open for 3% of the time, Pallas kernels for 4%

profile of v3, /device:TPU:1, one launch (start us, length us, event | category | flops | bytes accessed | tf_op | source)
XLA Modules:
  0.0 113.7 jit_solution(4434386208254474139)
XLA Ops:
  0.0 1.0 constant_dynamic-slice_fusion
  1.0 0.7 copy.17
  1.7 12.7 %all-to-all-start.1 = ((bf16[32,8,256]{2,1,0:T(8,128)(2,1)}), bf16[32,8,256]{2,1,0:T(8,128)(2,1)S(1)}, u32[]{:S(2)}, u32[]{:S(2)}) async-start(bf16[32,8,256]{2,1,0:T(8,128)(2,1)} %bitcast.11), calls=%async_computation.1 | async-start | bytes 262144 | tf_op jit(solution)/shard_map/all_to_all | solution.py:155
  14.4 0.0 copy-start.1
  14.5 2.8 %copy.16 = bf16[1,32,64,256]{3,1,2,0:T(8,128)(2,1)} copy(bf16[1,32,64,256]{3,2,1,0:T(8,128)(2,1)} %param.6) | data formatting | bytes 2097152 | tf_op args[1]
  17.2 7.7 %all-to-all-done.1.est0_ref = bf16[32,8,256]{2,1,0:T(8,128)(2,1)S(1)} async-done(((bf16[32,8,256]{2,1,0:T(8,128)(2,1)}), bf16[32,8,256]{2,1,0:T(8,128)(2,1)S(1)}, u32[]{:S(2)}, u32[]{:S(2)}) %all-to-all-start.1) | async-done | bytes 131104 | tf_op jit(solution)/shard_map/all_to_all | solution.py:155
  24.9 5.8 %all-to-all-start = ((bf16[64,32,256]{2,1,0:T(8,128)(2,1)}), bf16[64,32,256]{2,1,0:T(8,128)(2,1)S(1)}, u32[]{:S(2)}, u32[]{:S(2)}) async-start(bf16[64,32,256]{2,1,0:T(8,128)(2,1)} %bitcast.10), calls=%async_computation | async-start | bytes 2097152 | tf_op jit(solution)/shard_map/all_to_all | solution.py:157
  32.0 2.6 %collective-permute-start.4 = (bf16[32,8,256]{2,1,0:T(8,128)(2,1)S(1)}, bf16[32,8,256]{2,1,0:T(8,128)(2,1)S(1)}, u32[]{:S(2)}, u32[]{:S(2)}) collective-permute-start(bf16[32,8,256]{2,1,0:T(8,128)(2,1)S(1)} %all-to-all-done.1.est0_ref), channel_id=1, source_target_pairs={{0,96},{32,0},{64,32},{96,64},{1,97},{33,1},{65,33},{97,65},{2,98}... | collective-permute-start | bytes 393224 | tf_op jit(solution)/shard_map/ppermute | solution.py:161
  34.6 0.5 collective-permute-start.3
  35.1 0.6 collective-permute-start.2
  35.7 0.1 pad_add_fusion.1.own_ref
  35.8 1.6 %collective-permute-start = (s32[2]{0:T(128)S(1)}, s32[2]{0:T(128)S(1)}, u32[]{:S(2)}, u32[]{:S(2)}) collective-permute-start(s32[2]{0:T(128)S(1)} %pad_add_fusion.1.own_ref), channel_id=1, source_target_pairs={{0,128},{128,0},{1,129},{129,1},{2,130},{130,2},{3,131},{131,3},{4... | collective-permute-start | bytes 32 | tf_op jit(solution)/shard_map/ppermute | solution.py:150
  37.3 0.0 copy-done.1
  37.4 0.1 collective-permute-start.1
  37.5 0.1 pad_add_fusion.place_ref
  37.5 1.1 collective-permute-done.other_ref
  38.6 1.4 %collective-permute-done.1.other_profile_ref = f32[1,256]{1,0:T(1,128)S(1)} collective-permute-done((f32[1,256]{1,0:T(1,128)S(1)}, f32[1,256]{1,0:T(1,128)S(1)}, u32[]{:S(2)}, u32[]{:S(2)}) %collective-permute-start.1) | collective-permute-done | bytes 1056 | tf_op jit(solution)/shard_map/ppermute | solution.py:151
  40.1 0.0 collective-permute-done.4.est3_ref
  40.1 0.2 collective-permute-done.3.est2_ref
  40.3 4.0 %collective-permute-done.2.est1_ref = bf16[32,8,256]{2,1,0:T(8,128)(2,1)S(1)} collective-permute-done((bf16[32,8,256]{2,1,0:T(8,128)(2,1)S(1)}, bf16[32,8,256]{2,1,0:T(8,128)(2,1)S(1)}, u32[]{:S(2)}, u32[]{:S(2)}) %collective-permute-start.2) | collective-permute-done | bytes 131104 | tf_op jit(solution)/shard_map/ppermute | solution.py:161
  44.2 4.5 %forward_kernel.1 = (f32[2,1024,256]{2,1,0:T(8,128)S(1)}, bf16[2,256,256]{2,1,0:T(8,128)(2,1)S(1)}) custom-call(s32[2]{0:T(128)S(1)} %pad_add_fusion.place_ref, s32[2]{0:T(128)S(1)} %pad_add_fusion.1.own_ref, s32[2]{0:T(128)S(1)} %collective-permute-done.other_ref, f32[1,256]{1,0:T(1,128)S(1)} %copy-done.1, ...), custom_call_target="tpu_custom_call" | custom-call | flops 268435456 | bytes 8388608 | tf_op jit(solution)/shard_map/forward_kernel/pallas_call | solution.py:164
  48.7 10.6 %all-to-all-done.image_ref = bf16[64,32,256]{2,1,0:T(8,128)(2,1)S(1)} async-done(((bf16[64,32,256]{2,1,0:T(8,128)(2,1)}), bf16[64,32,256]{2,1,0:T(8,128)(2,1)S(1)}, u32[]{:S(2)}, u32[]{:S(2)}) %all-to-all-start) | async-done | bytes 1048608 | tf_op jit(solution)/shard_map/all_to_all | solution.py:157
  59.3 5.2 %back_kernel.1 = s16[4,32,8,256]{3,2,1,0:T(8,128)(2,1)S(1)} custom-call(s32[2]{0:T(128)S(1)} %pad_add_fusion.place_ref, s32[2]{0:T(128)S(1)} %pad_add_fusion.1.own_ref, s32[2]{0:T(128)S(1)} %collective-permute-done.other_ref, bf16[64,32,256]{2,1,0:T(8,128)(2,1)S(1)} %all-to-all-done.image_ref, f32[2,1024,256]{2,1,0:T(8,128)S(1)} %get-tuple-element.7.inverse_ref, ...), custom_call_target="tpu_custom_call" | custom-call | tf_op jit(solution)/shard_map/back_kernel/pallas_call | solution.py:179
  64.5 12.9 %all_to_all.25 = s16[4,32,8,256]{3,2,1,0:T(8,128)(2,1)S(1)} all-to-all(s16[4,32,8,256]{3,2,1,0:T(8,128)(2,1)S(1)} %back_kernel.1), channel_id=1, replica_groups=mesh['upper'=2,'column'=4,'tile'=32] {'column'}, dimensions={0} | all-to-all | bytes 1048576 | tf_op jit(solution)/shard_map/all_to_all | solution.py:188
  77.4 0.1 convert_reduce_fusion
  77.6 0.0 copy-start
  77.6 16.5 %all_to_all.26 = s16[32,8,256]{2,1,0:T(8,128)(2,1)S(1)} all-to-all(s16[32,8,256]{2,1,0:T(8,128)(2,1)S(1)} %shift-right-arithmetic_convert_fusion), channel_id=1, replica_groups=mesh['upper'=2,'column'=4,'tile'=32] {'tile'}, dimensions={0} | all-to-all | bytes 262144 | tf_op jit(solution)/shard_map/all_to_all | solution.py:191
  94.2 0.1 broadcast_in_dim.2
  94.3 17.3 %all_to_all.27 = s16[8,8,32,256]{3,2,1,0:T(8,128)(2,1)S(1)} all-to-all(s16[8,8,32,256]{3,2,1,0:T(8,128)(2,1)S(1)} %broadcast_in_dim.2), channel_id=1, replica_groups=mesh['upper'=2,'column'=4,'tile'=32] {'upper','column'}, dimensions={0} | all-to-all | bytes 2097152 | tf_op jit(solution)/shard_map/all_to_all | solution.py:193
  111.6 0.0 copy-done
  111.6 2.0 %final_kernel.1 = f32[32,64,256]{2,1,0:T(8,128)} custom-call(f32[32,64,256]{2,1,0:T(8,128)S(1)} %copy-done, s16[2,4,8,32,256]{4,3,2,1,0:T(8,128)(2,1)S(1)} %bitcast.12), custom_call_target="tpu_custom_call" | custom-call | tf_op jit(solution)/shard_map/final_kernel/pallas_call | solution.py:195
  (2 shorter events, 0.1 us)
Async XLA Ops:
  1.7 23.3 %all-to-all-start.1 = ((bf16[32,8,256]{2,1,0:T(8,128)(2,1)}), bf16[32,8,256]{2,1,0:T(8,128)(2,1)S(1)}, u32[]{:S(2)}, u32[]{:S(2)}) async-start(bf16[32,8,256]{2,1,0:T(8,128)(2,1)} %bitcast.11), calls=%async_computation.1 | async-start | bytes 262144 | tf_op jit(solution)/shard_map/all_to_all | solution.py:155
  14.4 22.9 %copy-start.1 = (f32[1,256]{1,0:T(1,128)S(1)}, f32[1,256]{1,0:T(1,128)}, u32[]{:S(2)}) copy-start(f32[1,256]{1,0:T(1,128)} %own_profile_ref.1) | copy-start | bytes 3076
  24.9 34.3 %all-to-all-start = ((bf16[64,32,256]{2,1,0:T(8,128)(2,1)}), bf16[64,32,256]{2,1,0:T(8,128)(2,1)S(1)}, u32[]{:S(2)}, u32[]{:S(2)}) async-start(bf16[64,32,256]{2,1,0:T(8,128)(2,1)} %bitcast.10), calls=%async_computation | async-start | bytes 2097152 | tf_op jit(solution)/shard_map/all_to_all | solution.py:157
  32.0 8.1 %collective-permute-start.4 = (bf16[32,8,256]{2,1,0:T(8,128)(2,1)S(1)}, bf16[32,8,256]{2,1,0:T(8,128)(2,1)S(1)}, u32[]{:S(2)}, u32[]{:S(2)}) collective-permute-start(bf16[32,8,256]{2,1,0:T(8,128)(2,1)S(1)} %all-to-all-done.1.est0_ref), channel_id=1, source_target_pairs={{0,96},{32,0},{64,32},{96,64},{1,97},{33,1},{65,33},{97,65},{2,98}... | collective-permute-start | bytes 393224 | tf_op jit(solution)/shard_map/ppermute | solution.py:161
  34.6 5.7 %collective-permute-start.3 = (bf16[32,8,256]{2,1,0:T(8,128)(2,1)S(1)}, bf16[32,8,256]{2,1,0:T(8,128)(2,1)S(1)}, u32[]{:S(2)}, u32[]{:S(2)}) collective-permute-start(bf16[32,8,256]{2,1,0:T(8,128)(2,1)S(1)} %all-to-all-done.1.est0_ref), channel_id=1, source_target_pairs={{0,64},{32,96},{64,0},{96,32},{1,65},{33,97},{65,1},{97,33},{2,66}... | collective-permute-start | bytes 393224 | tf_op jit(solution)/shard_map/ppermute | solution.py:161
  35.1 9.2 %collective-permute-start.2 = (bf16[32,8,256]{2,1,0:T(8,128)(2,1)S(1)}, bf16[32,8,256]{2,1,0:T(8,128)(2,1)S(1)}, u32[]{:S(2)}, u32[]{:S(2)}) collective-permute-start(bf16[32,8,256]{2,1,0:T(8,128)(2,1)S(1)} %all-to-all-done.1.est0_ref), channel_id=1, source_target_pairs={{0,32},{32,64},{64,96},{96,0},{1,33},{33,65},{65,97},{97,1},{2,34}... | collective-permute-start | bytes 393224 | tf_op jit(solution)/shard_map/ppermute | solution.py:161
  35.8 2.9 %collective-permute-start = (s32[2]{0:T(128)S(1)}, s32[2]{0:T(128)S(1)}, u32[]{:S(2)}, u32[]{:S(2)}) collective-permute-start(s32[2]{0:T(128)S(1)} %pad_add_fusion.1.own_ref), channel_id=1, source_target_pairs={{0,128},{128,0},{1,129},{129,1},{2,130},{130,2},{3,131},{131,3},{4... | collective-permute-start | bytes 32 | tf_op jit(solution)/shard_map/ppermute | solution.py:150
  37.4 2.7 %collective-permute-start.1 = (f32[1,256]{1,0:T(1,128)S(1)}, f32[1,256]{1,0:T(1,128)S(1)}, u32[]{:S(2)}, u32[]{:S(2)}) collective-permute-start(f32[1,256]{1,0:T(1,128)S(1)} %copy-done.1), channel_id=1, source_target_pairs={{0,128},{128,0},{1,129},{129,1},{2,130},{130,2},{3,131},{131,3},{4... | collective-permute-start | bytes 3080 | tf_op jit(solution)/shard_map/ppermute | solution.py:151
  77.6 34.0 %copy-start = (f32[32,64,256]{2,1,0:T(8,128)S(1)}, f32[32,64,256]{2,1,0:T(8,128)}, u32[]{:S(2)}) copy-start(f32[32,64,256]{2,1,0:T(8,128)} %est_ref.1) | copy-start | bytes 6291460
